TPU v7x, 512 devices: a whole 4x8x8 slice. The times are simulated.
512 devices in a mesh: vec: 16 (over y, x_hi), amp: 32 (over x_lo, z, core).
Axes of the slice: x: 4 (x_hi: 2, x_lo: 2; x = x_hi * 2 + x_lo), y: 8, z: 8, core: 2. Of those that a mesh axis runs over, the one named last changes fastest.
Arguments:
- chol: bfloat16 [64, 1024, 8192], P(None, 'amp', 'vec'), may hold values from -2.5 to 2.5
- amplitudes: bfloat16 [64, 256, 1024], P(None, 'amp'), may hold values from -0.125 to 0.125
- task_list: int32 [64, 4], replicated, may hold values from 0 to 63
- counts: int32 [32], replicated, may hold values from 0 to 2, as said below
Outputs:
- residual: bfloat16 [64, 256, 1024], P('vec', 'amp')
Inputs may be any that keep to these rules, and one draw needn't show every extreme that they name: The counts sum to 32, and one of them equals 2.
All inputs are finite; a program needn't handle non-finite values.
Results may differ from a plain program's by a relative error of at most 0.0055.
Values may be sent and summed in bfloat16 or wider, within the bound.
A program may use at most 128 MiB of HBM per device.

v0:
```python
import jax
import jax.numpy as jnp
from jax import lax
from jax.sharding import PartitionSpec as P

VB = 32
PAIRS = 1024
MOST = 2


def integral_tile(x_rows, y_rows):
    products = lax.dot_general(
        x_rows, y_rows, (((1,), (1,)), ((), ())), preferred_element_type=jnp.float32
    )
    return (
        products.reshape(VB, VB, VB, VB)
        .transpose(0, 2, 1, 3)
        .reshape(PAIRS, PAIRS)
        .astype(jnp.bfloat16)
    )


def task_term(x_rows, y_rows, amp_rows):
    integral = integral_tile(x_rows, y_rows)
    products = lax.dot_general(
        amp_rows, integral, (((1,), (1,)), ((), ())), preferred_element_type=jnp.float32
    )
    return products.astype(jnp.bfloat16)


def contract_slots(pieces):
    return jax.vmap(task_term)(pieces[0], pieces[1], pieces[2])


def listed_entries(counts, owners):
    slot_ids = jnp.arange(MOST, dtype=jnp.int32)[:, None]
    lists = jnp.arange(owners, dtype=jnp.int32)[None, :]
    return (lists * MOST + slot_ids, slot_ids < counts[None, :])


def local(chol, amplitudes, task_list, counts):
    owners = lax.axis_size("amp")
    entries, live_slots = listed_entries(counts, owners)
    fields = task_list[entries]
    slot_count = entries.shape[0]
    x_send = jnp.take(chol, fields[:, :, 0], axis=0).reshape(slot_count, -1, chol.shape[2])
    y_send = jnp.take(chol, fields[:, :, 1], axis=0).reshape(slot_count, -1, chol.shape[2])
    amp_send = jnp.take(amplitudes, fields[:, :, 2], axis=0).reshape(
        slot_count, -1, amplitudes.shape[2]
    )
    results = contract_slots(
        (
            lax.all_to_all(x_send, "amp", split_axis=1, concat_axis=1, tiled=True),
            lax.all_to_all(y_send, "amp", split_axis=1, concat_axis=1, tiled=True),
            lax.all_to_all(amp_send, "amp", split_axis=1, concat_axis=1, tiled=True),
        )
    )
    returned = lax.all_to_all(results, "amp", split_axis=1, concat_axis=0, tiled=True)
    targets = fields[:, :, 3].T.reshape(-1)
    live_flat = live_slots.T.reshape(-1)
    tiles = amplitudes.shape[0]
    selector = (
        (jnp.arange(tiles, dtype=jnp.int32)[:, None] == targets[None, :]) & live_flat[None, :]
    ).astype(jnp.bfloat16)
    summed = jnp.dot(
        selector, returned.reshape(returned.shape[0], -1), preferred_element_type=jnp.float32
    )
    summed = summed.reshape(tiles, returned.shape[1], returned.shape[2])
    share = lax.psum_scatter(summed, "vec", scatter_dimension=0, tiled=True)
    return share.astype(jnp.bfloat16)


def solution(mesh):
    placed = (P(None, "amp", "vec"), P(None, "amp", None), P(), P())
    return jax.shard_map(
        local, mesh=mesh, in_specs=placed, out_specs=P("vec", "amp", None), check_vma=False
    )
```

profile of v0, /device:TPU:1, one launch (start us, length us, event | category | flops | bytes accessed | tf_op | source)
XLA Modules:
  0.0 468.5 jit_solution(3625914887709408839)
XLA Ops:
  6.5 0.0 copy-start
  6.5 0.9 copy.42
  7.5 0.1 reshape.108
  7.6 0.6 gather_fusion
  8.2 0.1 fusion.11
  8.2 0.1 copy.64
  8.4 0.1 copy.51
  8.5 0.1 reshape.133
  8.5 0.0 copy-done
  8.6 2.0 gather_fusion.3
  10.6 5.4 %broadcast_select_fusion = bf16[2,32,32,512]{3,0,2,1:T(2,128)(2,1)} fusion(pred[2,32]{0,1:T(8,128)(4,1)S(1)} %copy.51, bf16[2,32,32,512]{3,2,1,0:T(8,128)(2,1)} %bitcast.47), kind=kLoop, calls=%fused_computation.4 | loop fusion | flops 1048576 | bytes 4194368 | tf_op jit(solution)/shard_map/jit(_take)/select_n | solution.py:47
  16.0 12.9 %all-to-all-start.2 = ((bf16[2,1024,512]{2,0,1:T(2,128)(2,1)}), bf16[2,1024,512]{2,0,1:T(2,128)(2,1)}, u32[]{:S(2)}, u32[]{:S(2)}) async-start(bf16[2,1024,512]{2,0,1:T(2,128)(2,1)} %bitcast.49), calls=%async_computation.2 | async-start | bytes 4194304 | tf_op jit(solution)/shard_map/all_to_all | solution.py:54
  28.9 0.1 copy.63
  29.0 0.1 copy.48
  29.1 0.1 reshape.129
  29.2 2.0 gather_fusion.2
  31.3 5.5 %broadcast_select_fusion.1 = bf16[2,32,32,512]{3,0,2,1:T(2,128)(2,1)} fusion(pred[2,32]{0,1:T(8,128)(4,1)S(1)} %copy.48, bf16[2,32,32,512]{3,2,1,0:T(8,128)(2,1)} %bitcast.48), kind=kLoop, calls=%fused_computation.5 | loop fusion | flops 1048576 | bytes 4194368 | tf_op jit(solution)/shard_map/jit(_take)/select_n | solution.py:46
  36.7 41.5 %all-to-all-done.2 = bf16[2,1024,512]{2,0,1:T(2,128)(2,1)} async-done(((bf16[2,1024,512]{2,0,1:T(2,128)(2,1)}), bf16[2,1024,512]{2,0,1:T(2,128)(2,1)}, u32[]{:S(2)}, u32[]{:S(2)}) %all-to-all-start.2) | async-done | bytes 2097184 | tf_op jit(solution)/shard_map/all_to_all | solution.py:54
  78.2 0.0 copy-start.2
  78.2 5.8 %all-to-all-start.1 = ((bf16[2,1024,512]{2,0,1:T(2,128)(2,1)}), bf16[2,1024,512]{2,0,1:T(2,128)(2,1)}, u32[]{:S(2)}, u32[]{:S(2)}) async-start(bf16[2,1024,512]{2,0,1:T(2,128)(2,1)} %bitcast.8), calls=%async_computation.1 | async-start | bytes 4194304 | tf_op jit(solution)/shard_map/all_to_all | solution.py:53
  84.1 0.1 copy.62
  84.2 0.1 broadcast_in_dim.28
  84.3 0.1 broadcast_in_dim.29
  84.4 0.1 reshape.116
  84.5 0.0 copy-done.2
  84.5 0.6 gather_fusion.1
  85.1 0.2 bitcast_select_fusion
  85.3 2.1 copy.46
  87.3 46.1 %all-to-all-done.1 = bf16[2,1024,512]{2,0,1:T(2,128)(2,1)} async-done(((bf16[2,1024,512]{2,0,1:T(2,128)(2,1)}), bf16[2,1024,512]{2,0,1:T(2,128)(2,1)}, u32[]{:S(2)}, u32[]{:S(2)}) %all-to-all-start.1) | async-done | bytes 2097184 | tf_op jit(solution)/shard_map/all_to_all | solution.py:53
  133.5 5.6 %all-to-all-start = ((bf16[2,256,1024]{2,0,1:T(2,128)(2,1)}), bf16[2,256,1024]{2,0,1:T(2,128)(2,1)S(1)}, u32[]{:S(2)}, u32[]{:S(2)}) async-start(bf16[2,256,1024]{2,0,1:T(2,128)(2,1)} %copy.46), calls=%async_computation | async-start | bytes 2097152 | tf_op jit(solution)/shard_map/all_to_all | solution.py:55
  139.1 6.5 %convolution_convert_fusion = bf16[2,1024,1024]{2,1,0:T(8,128)(2,1)} fusion(bf16[2,1024,512]{2,0,1:T(2,128)(2,1)} %all-to-all-done.2, bf16[2,1024,512]{2,0,1:T(2,128)(2,1)} %all-to-all-done.1), kind=kOutput, calls=%fused_computation.6 | convolution fusion | flops 2149580800 | bytes 8388608 | tf_op jit(solution)/shard_map/vmap()/dot_general | solution.py:12
  145.7 20.3 %convert_element_type.20 = bf16[2,32,32,32,32]{4,3,2,1,0:T(8,128)(2,1)} reshape(bf16[2,1024,1024]{2,1,0:T(8,128)(2,1)} %convolution_convert_fusion) | data formatting | bytes 8388608 | tf_op jit(solution)/shard_map/vmap()/convert_element_type | solution.py:19
  166.0 17.5 %copy.55 = bf16[2,32,32,32,32]{4,3,2,1,0:T(8,128)(2,1)} copy(bf16[2,32,32,32,32]{4,2,3,1,0:T(8,128)(2,1)} %bitcast.46) | data formatting | bytes 8388608 | tf_op jit(solution)/shard_map/vmap()/convert_element_type | solution.py:19
  183.5 23.2 %convert_element_type.22 = bf16[2,1024,1024]{2,1,0:T(8,128)(2,1)} reshape(bf16[2,32,32,32,32]{4,3,2,1,0:T(8,128)(2,1)} %copy.55) | data formatting | bytes 8388608 | tf_op jit(solution)/shard_map/vmap()/convert_element_type | solution.py:19
  206.7 0.0 all-to-all-done
  206.7 3.5 convolution_convert_fusion.1
  210.2 0.0 copy-start.3
  210.2 2.1 copy.57
  212.3 8.3 %all-to-all-start.3 = ((bf16[2,256,1024]{2,0,1:T(2,128)(2,1)}), bf16[2,256,1024]{2,0,1:T(2,128)(2,1)S(1)}, u32[]{:S(2)}, u32[]{:S(2)}) async-start(bf16[2,256,1024]{2,0,1:T(2,128)(2,1)} %copy.57), calls=%async_computation.3 | async-start | bytes 2097152 | tf_op jit(solution)/shard_map/all_to_all | solution.py:58
  220.6 0.0 reduce-scatter.2.cloned.1.call-start
  220.7 0.1 copy.61
  220.7 0.1 copy.44
  220.8 0.1 eq.16
  220.9 0.0 copy-done.3
  220.9 0.1 iota_compare_fusion.1
  221.0 0.1 lt.50
  221.1 26.0 %all-to-all-done.3 = bf16[2,256,1024]{2,0,1:T(2,128)(2,1)S(1)} async-done(((bf16[2,256,1024]{2,0,1:T(2,128)(2,1)}), bf16[2,256,1024]{2,0,1:T(2,128)(2,1)S(1)}, u32[]{:S(2)}, u32[]{:S(2)}) %all-to-all-start.3) | async-done | bytes 1048608 | tf_op jit(solution)/shard_map/all_to_all | solution.py:58
  247.1 0.3 copy.58
  247.4 1.4 fusion.2
  248.8 0.0 copy-start.1
  248.8 2.5 copy.60
  251.4 0.0 reduce-scatter.2.cloned.1.call-update
  251.4 208.7 %reduce-scatter.2.cloned.1.call-done = f32[4,8,1024]{2,1,0:T(8,128)} async-done(((f32[64,8,1024]{2,1,0:T(8,128)}), f32[4,8,1024]{2,1,0:T(8,128)}) %reduce-scatter.2.cloned.1.call-update) | async-done | bytes 131088 | tf_op jit(solution)/shard_map/reduce_scatter | solution.py:69
  460.1 1.5 convert_element_type.24
  461.7 0.0 copy-done.1
  (12 shorter events, 0.1 us)
Async XLA Ops:
  6.5 2.0 copy-start
  16.0 62.3 %all-to-all-start.2 = ((bf16[2,1024,512]{2,0,1:T(2,128)(2,1)}), bf16[2,1024,512]{2,0,1:T(2,128)(2,1)}, u32[]{:S(2)}, u32[]{:S(2)}) async-start(bf16[2,1024,512]{2,0,1:T(2,128)(2,1)} %bitcast.49), calls=%async_computation.2 | async-start | bytes 4194304 | tf_op jit(solution)/shard_map/all_to_all | solution.py:54
  78.2 6.2 %copy-start.2 = (bf16[64,8,1024]{2,1,0:T(8,128)(2,1)S(1)}, bf16[64,8,1024]{2,1,0:T(8,128)(2,1)}, u32[]{:S(2)}) copy-start(bf16[64,8,1024]{2,1,0:T(8,128)(2,1)} %param.7) | copy-start | bytes 3145732
  78.2 55.2 %all-to-all-start.1 = ((bf16[2,1024,512]{2,0,1:T(2,128)(2,1)}), bf16[2,1024,512]{2,0,1:T(2,128)(2,1)}, u32[]{:S(2)}, u32[]{:S(2)}) async-start(bf16[2,1024,512]{2,0,1:T(2,128)(2,1)} %bitcast.8), calls=%async_computation.1 | async-start | bytes 4194304 | tf_op jit(solution)/shard_map/all_to_all | solution.py:53
  133.5 73.2 %all-to-all-start = ((bf16[2,256,1024]{2,0,1:T(2,128)(2,1)}), bf16[2,256,1024]{2,0,1:T(2,128)(2,1)S(1)}, u32[]{:S(2)}, u32[]{:S(2)}) async-start(bf16[2,256,1024]{2,0,1:T(2,128)(2,1)} %copy.46), calls=%async_computation | async-start | bytes 2097152 | tf_op jit(solution)/shard_map/all_to_all | solution.py:55
  210.2 10.7 %copy-start.3 = (s32[32]{0:T(128)S(1)}, s32[32]{0:T(128)}, u32[]{:S(2)}) copy-start(s32[32]{0:T(128)} %param.9) | copy-start | bytes 388
  212.3 34.8 %all-to-all-start.3 = ((bf16[2,256,1024]{2,0,1:T(2,128)(2,1)}), bf16[2,256,1024]{2,0,1:T(2,128)(2,1)S(1)}, u32[]{:S(2)}, u32[]{:S(2)}) async-start(bf16[2,256,1024]{2,0,1:T(2,128)(2,1)} %copy.57), calls=%async_computation.3 | async-start | bytes 2097152 | tf_op jit(solution)/shard_map/all_to_all | solution.py:58
  220.6 239.5 %reduce-scatter.2.cloned.1.call-start = ((), (), s32[]{:S(2)}) async-start(), calls=%async_computation.5 | async-start | bytes 2228224 | tf_op jit(solution)/shard_map/reduce_scatter | solution.py:69
  248.8 212.8 %copy-start.1 = (bf16[64,32,512]{2,1,0:T(8,128)(2,1)S(1)}, bf16[64,32,512]{2,1,0:T(8,128)(2,1)}, u32[]{:S(2)}) copy-start(bf16[64,32,512]{2,1,0:T(8,128)(2,1)} %param.6) | copy-start | bytes 6291460
Sparse Core Ops, SparseCore 0:
  251.5 208.5 reduce-scatter.1
where the time goes:
time: 474 us; the launch traced here: 469 us
  waiting for transfers between devices  322 us (68%)
  local copies, waits for them, and re-layouts  75.6 us (16%)
  starting transfers between devices  32.8 us (7%)
  between operations  13.5 us (3%)
  other arithmetic  12.8 us (3%)
  matrix products  11.5 us (2%)
    reduce_scatter x1, waiting for transfers between devices, local(): share = lax.psum_scatter(summed, 'vec', scatter_dimension=0, tiled=True)  209 us
    convert_element_type x3, local copies, waits for them, and re-layouts, integral_tile(): return products.reshape(VB, VB, VB, VB).transpose(0, 2, 1, 3).reshape(PAI...  61 us
    all_to_all x1, waiting for transfers between devices, local(): lax.all_to_all(x_send, 'amp', split_axis=1, concat_axis=1, tiled=True)  46.1 us
    all_to_all x1, waiting for transfers between devices, local(): lax.all_to_all(y_send, 'amp', split_axis=1, concat_axis=1, tiled=True)  41.5 us
    all_to_all x1, waiting for transfers between devices, local(): lax.all_to_all(results, 'amp', split_axis=1, concat_axis=0, tiled=True)  26 us
    all_to_all x1, starting transfers between devices, local(): lax.all_to_all(y_send, 'amp', split_axis=1, concat_axis=1, tiled=True)  12.9 us
  transfers between devices with their start and end apart: 5, of which 4 were waited for; matrix products, arithmetic and copies ran while one was open for 17% of the time, Pallas kernels for 0%

commit v1 on v0

v1 whole, which is shorter than its diff:
```python
import jax
import jax.numpy as jnp
from jax import lax
from jax.experimental import pallas as pl
from jax.experimental.pallas import tpu as pltpu
from jax.sharding import PartitionSpec as P

VB = 32
PAIRS = 1024
MOST = 2
TASKS = 32
N_AMP = 32
N_VEC = 16
MESH = pl.DeviceIdType.MESH
F32 = jnp.float32
BF16 = jnp.bfloat16
NT = (((1,), (1,)), ((), ()))


def compact_kernel(list_ref, counts_ref, out_ref):
    def entry(e, position):
        for k in range(4):
            out_ref[position * 4 + k] = list_ref[e, k]
        return position + jnp.where(lax.rem(e, MOST) < counts_ref[e // MOST], 1, 0)

    lax.fori_loop(0, N_AMP * MOST, entry, 0)


def compact(task_list, counts):
    return pl.pallas_call(
        compact_kernel,
        out_shape=jax.ShapeDtypeStruct(((TASKS + 1) * 4,), jnp.int32),
        in_specs=[pl.BlockSpec(memory_space=pltpu.SMEM)] * 2,
        out_specs=pl.BlockSpec(memory_space=pltpu.SMEM),
    )(task_list, counts)


def shift_of(q):
    return ((q + 1) // 2) * (2 * (q % 2) - 1)


def arrived(block, sem):
    pltpu.make_async_copy(block, block, sem).wait()


def ladder_kernel(
    task_ref, chol_hbm, amp_hbm, out_ref,
    chol_v, amp_v, xs, ys, ts, xr, yr, tr, xp, tfull, qs, vs, vr, ssum, keys, s2s, s2r, s3s, s3r,
    in_sem, x_send, x_recv, y_send, y_recv, t_send, t_recv, tv_send, tv_recv,
    v_send, v_recv, s2_send, s2_recv, s3_send, s3_recv,
):
    v = lax.axis_index("vec")
    m = lax.axis_index("amp")
    y, x_hi = v // 2, v % 2
    x_lo, z, core = m // 16, (m // 2) % 8, m % 2

    def amp_peer(j):
        return ((x_lo + (j // 2) % 2) % 2) * 16 + ((z + shift_of(j // 4) + 8) % 8) * 2 + (core + j) % 2

    def vec_peer(j):
        return (v + j) % N_VEC

    def to_amp(src, dst, send, recv, peer):
        pltpu.make_async_remote_copy(
            src_ref=src, dst_ref=dst, send_sem=send, recv_sem=recv,
            device_id={"amp": peer}, device_id_type=MESH,
        ).start()

    def to_vec(src, dst, send, recv, peer):
        pltpu.make_async_remote_copy(
            src_ref=src, dst_ref=dst, send_sem=send, recv_sem=recv,
            device_id={"vec": peer}, device_id_type=MESH,
        ).start()

    load_amp = pltpu.make_async_copy(amp_hbm, amp_v, in_sem.at[0])
    load_chol = pltpu.make_async_copy(chol_hbm, chol_v, in_sem.at[1])
    load_amp.start()
    load_chol.start()

    barrier = pltpu.get_barrier_semaphore()

    @pl.loop(1, N_AMP)
    def _(j):
        pl.semaphore_signal(barrier, inc=1, device_id={"amp": amp_peer(j)}, device_id_type=MESH)

    @pl.loop(1, N_VEC)
    def _(j):
        pl.semaphore_signal(barrier, inc=1, device_id={"vec": vec_peer(j)}, device_id_type=MESH)

    load_amp.wait()
    columns = pl.ds(pl.multiple_of(y * 128, 128), 128)

    @pl.loop(0, TASKS)
    def _(t):
        ts[t] = amp_v[task_ref[t * 4 + 2], :, columns]

    load_chol.wait()

    @pl.loop(0, TASKS)
    def _(t):
        xs[t] = chol_v[task_ref[t * 4]]
        ys[t] = chol_v[task_ref[t * 4 + 1]]

    pl.semaphore_wait(barrier, N_AMP + N_VEC - 2)

    @pl.when(core == x_hi)
    def _():
        pltpu.make_async_copy(ts.at[m], tr.at[v, m // 2], t_recv).start()

        @pl.loop(1, N_AMP)
        def _(j):
            peer = amp_peer(j)
            to_amp(ts.at[peer], tr.at[v, m // 2], t_send, t_recv, peer)

    pltpu.make_async_copy(xs.at[m], xr.at[m], x_recv).start()

    @pl.loop(1, N_AMP)
    def _(j):
        peer = amp_peer(j)
        to_amp(xs.at[peer], xr.at[m], x_send, x_recv, peer)

    pltpu.make_async_copy(ys.at[m], yr.at[x_lo, z, core], y_recv.at[0]).start()

    @pl.loop(1, N_AMP)
    def _(j):
        peer = amp_peer(j)
        to_amp(ys.at[peer], yr.at[x_lo, z, core], y_send, y_recv.at[j // 4], peer)

    arrived(tr.at[v], t_recv)

    @pl.loop(1, N_VEC)
    def _(j):
        to_vec(tr.at[v], tr.at[v], tv_send, tv_recv, vec_peer(j))

    lane = lax.broadcasted_iota(jnp.int32, (8, 256), 1)

    def place(t, held):
        return jnp.where(lane // 8 == t, task_ref[t * 4 + 3] * 8 + lane % 8, held)

    wanted = lax.fori_loop(0, TASKS, place, jnp.zeros((8, 256), jnp.int32))[:1]

    @pl.loop(0, 4)
    def _(k):
        rows = lax.broadcasted_iota(jnp.int32, (128, 256), 0) + k * 128
        keys[pl.ds(pl.multiple_of(k * 128, 128), 128), :] = jnp.where(rows == wanted, 1.0, 0.0).astype(BF16)

    arrived(xr, x_recv)

    @pl.loop(0, 8)
    def _(k):
        rows = lax.broadcasted_iota(jnp.int32, (128, 1024), 0) + k * 128
        cols = lax.broadcasted_iota(jnp.int32, (128, 1024), 1)
        pick = jnp.where(cols == (rows % 32) * 32 + rows // 32, 1.0, 0.0).astype(BF16)
        xp[pl.ds(pl.multiple_of(k * 128, 128), 128), :] = jnp.dot(
            pick, xr[...].reshape(PAIRS, 512), preferred_element_type=F32
        ).astype(BF16)

    arrived(tr.at[pl.ds(0, N_VEC - 1)], tv_recv)

    @pl.loop(0, 16)
    def _(k):
        for c in range(8):
            both = [
                jnp.concatenate([tr[2 * c, k].astype(F32), tr[2 * c + 1, k].astype(F32)], axis=0)
            ]
            tfull[pl.ds(pl.multiple_of(k * 16, 16), 16), c * 128 : c * 128 + 128] = both[0].astype(BF16)

    lanes = lax.broadcasted_iota(jnp.int32, (32, 128), 1)
    low_half = lanes < 64
    even = (lanes // 32) % 2 == 0

    @pl.loop(0, 8)
    def _(q):
        from_z = (z - shift_of(q) + 8) % 8
        arrived(yr.at[0, pl.ds(0, 2)], y_recv.at[q])
        y_rows = jnp.concatenate(
            [yr[0, from_z].reshape(64, 512), yr[1, from_z].reshape(64, 512)], axis=0
        )
        for k in range(8):
            block = lax.dot_general(
                xp[k * 128 : k * 128 + 128, :], y_rows, NT, preferred_element_type=F32
            )
            p0, p1, p2, p3 = (block[c * 32 : c * 32 + 32] for c in range(4))
            a0 = jnp.where(low_half, p0, pltpu.roll(p2, 64, 1))
            a2 = jnp.where(low_half, pltpu.roll(p0, 64, 1), p2)
            a1 = jnp.where(low_half, p1, pltpu.roll(p3, 64, 1))
            a3 = jnp.where(low_half, pltpu.roll(p1, 64, 1), p3)
            w = (
                jnp.where(even, a0, pltpu.roll(a1, 32, 1)),
                jnp.where(even, pltpu.roll(a0, 96, 1), a1),
                jnp.where(even, a2, pltpu.roll(a3, 32, 1)),
                jnp.where(even, pltpu.roll(a2, 96, 1), a3),
            )
            for b in range(4):
                qs[b * 32 : b * 32 + 32, k * 128 : k * 128 + 128] = w[b].astype(BF16)
        term = lax.dot_general(qs[...], tfull[...], NT, preferred_element_type=F32)
        for k in range(N_VEC):
            vs[q, k] = term[k * 8 : k * 8 + 8].astype(BF16)

        pltpu.make_async_copy(vs.at[q, v], vr.at[q, v], v_recv.at[q]).start()

        @pl.loop(1, N_VEC)
        def _(j):
            peer = vec_peer(j)
            to_vec(vs.at[q, peer], vr.at[q, v], v_send.at[q], v_recv.at[q], peer)

    @pl.loop(0, 8)
    def _(q):
        from_z = (z - shift_of(q) + 8) % 8
        arrived(vr.at[q], v_recv.at[q])
        total = vr[q, 0].astype(F32)
        for k in range(1, N_VEC):
            total += vr[q, k].astype(F32)
        high = total.astype(BF16).astype(F32)
        ssum[pl.ds(pl.multiple_of(from_z * 8, 8), 8), :] = high
        ssum[pl.ds(pl.multiple_of(from_z * 8 + 64, 8), 8), :] = total - high

    turned = ssum[...].T
    for k in range(N_AMP):
        s2s[k] = turned[k * 8 : k * 8 + 8].astype(BF16)

    pltpu.make_async_copy(s2s.at[m], s2r.at[m], s2_recv).start()

    @pl.loop(1, N_AMP)
    def _(j):
        peer = amp_peer(j)
        to_amp(s2s.at[peer], s2r.at[m], s2_send, s2_recv, peer)

    arrived(s2r, s2_recv)
    parts = s2r[...].astype(F32).reshape(256, 128).astype(BF16)
    tiles = jnp.dot(keys[...], parts, preferred_element_type=F32)
    tiles = tiles + pltpu.roll(tiles, 64, 1)
    low16 = lax.broadcasted_iota(jnp.int32, (16, 128), 1) < 64
    for k in range(N_VEC):
        s3s[k] = jnp.where(
            low16, tiles[k * 32 : k * 32 + 16], tiles[k * 32 + 16 : k * 32 + 32]
        ).astype(BF16)

    pltpu.make_async_copy(s3s.at[v], s3r.at[v], s3_recv).start()

    @pl.loop(1, N_VEC)
    def _(j):
        peer = vec_peer(j)
        to_vec(s3s.at[peer], s3r.at[v], s3_send, s3_recv, peer)

    arrived(s3r, s3_recv)
    out_ref[...] = s3r[...]

    @pl.when(core == x_hi)
    def _():
        arrived(ts.at[pl.ds(0, N_AMP - 1)], t_send)

    arrived(xs.at[pl.ds(0, N_AMP - 1)], x_send)
    arrived(ys.at[pl.ds(0, N_AMP - 1)], y_send)
    arrived(tr.at[pl.ds(0, N_VEC - 1)], tv_send)

    @pl.loop(0, 8)
    def _(q):
        arrived(vs.at[q, pl.ds(0, N_VEC - 1)], v_send.at[q])

    arrived(s2s.at[pl.ds(0, N_AMP - 1)], s2_send)
    arrived(s3s.at[pl.ds(0, N_VEC - 1)], s3_send)


def ladder(tasks, chol, amplitudes):
    dma = pltpu.SemaphoreType.DMA
    return pl.pallas_call(
        ladder_kernel,
        out_shape=jax.ShapeDtypeStruct((N_VEC, 16, 128), BF16),
        in_specs=[
            pl.BlockSpec(memory_space=pltpu.SMEM),
            pl.BlockSpec(memory_space=pl.ANY),
            pl.BlockSpec(memory_space=pl.ANY),
        ],
        out_specs=pl.BlockSpec(memory_space=pltpu.VMEM),
        scratch_shapes=[
            pltpu.VMEM((64, 32, 512), BF16),
            pltpu.VMEM((64, 8, 1024), BF16),
            pltpu.VMEM((32, 32, 512), BF16),
            pltpu.VMEM((32, 32, 512), BF16),
            pltpu.VMEM((32, 8, 128), BF16),
            pltpu.VMEM((32, 32, 512), BF16),
            pltpu.VMEM((2, 8, 2, 32, 512), BF16),
            pltpu.VMEM((16, 16, 8, 128), BF16),
            pltpu.VMEM((1024, 512), BF16),
            pltpu.VMEM((256, 1024), BF16),
            pltpu.VMEM((128, 1024), BF16),
            pltpu.VMEM((8, 16, 8, 256), BF16),
            pltpu.VMEM((8, 16, 8, 256), BF16),
            pltpu.VMEM((128, 256), F32),
            pltpu.VMEM((512, 256), BF16),
            pltpu.VMEM((32, 8, 128), BF16),
            pltpu.VMEM((32, 8, 128), BF16),
            pltpu.VMEM((16, 16, 128), BF16),
            pltpu.VMEM((16, 16, 128), BF16),
            dma((2,)),
            dma(()), dma(()),
            dma(()), dma((8,)),
            dma(()), dma(()),
            dma(()), dma(()),
            dma((8,)), dma((8,)),
            dma(()), dma(()),
            dma(()), dma(()),
        ],
        compiler_params=pltpu.CompilerParams(collective_id=0, has_side_effects=True),
    )(tasks, chol, amplitudes)


def local(chol, amplitudes, task_list, counts):
    tasks = compact(task_list, counts)
    got = ladder(tasks, chol, amplitudes)
    got = got.reshape(2, 2, 4, 2, 8, 2, 8, 8)
    return got.transpose(5, 3, 4, 2, 7, 0, 6, 1).reshape(4, 8, PAIRS)


def solution(mesh):
    placed = (P(None, "amp", "vec"), P(None, "amp", None), P(), P())
    return jax.shard_map(
        local, mesh=mesh, in_specs=placed, out_specs=P("vec", "amp", None), check_vma=False
    )
```

time: 474 us -> 98.1 us (0.21); the launches traced: 469 us -> 97.5 us
  waiting for transfers between devices: 322 us -> 0 us
  Pallas kernels: 0 us -> 90.8 us
  local copies, waits for them, and re-layouts: 75.6 us -> 6.69 us
  starting transfers between devices: 32.8 us -> 0 us
  between operations: 13.5 us -> 0.03 us
  other arithmetic: 12.8 us -> 0 us
  matrix products: 11.5 us -> 0 us
    reduce_scatter x1 -> x0, waiting for transfers between devices: 209 us -> none  [local(): share = lax.psum_scatter(summed, 'vec', scatter_dimension=0, tiled=True)]
    all_to_all x4 -> x0, waiting for transfers between devices: 114 us -> none  [the longest x1 46.1 us: local(): lax.all_to_all(x_send, 'amp', split_axis=1, concat_axis=1, tiled=True)]
    pallas_call x0 -> x2, Pallas kernels: none -> 90.8 us  [the longest x1 88 us: ladder(): pl.pallas_call(ladder_kernel, out_shape=jax.ShapeDtypeStruct((N_VEC, 16,...]
    convert_element_type x4 -> x0, local copies, waits for them, and re-layouts: 63.1 us -> none  [the longest x3 61 us: integral_tile(): return products.reshape(VB, VB, VB, VB).transpose(0, 2, 1, 3).reshape(PAI...]
    all_to_all x4 -> x0, starting transfers between devices: 32.7 us -> none  [the longest x1 12.9 us: local(): lax.all_to_all(y_send, 'amp', split_axis=1, concat_axis=1, tiled=True)]
    dot_general x3 -> x0, matrix products: 11.5 us -> none  [the longest x1 6.54 us: integral_tile(): lax.dot_general(x_rows, y_rows, (((1,), (1,)), ((), ())), preferred_eleme...]
    select_n x7 -> x0, other arithmetic: 11.1 us -> none  [the longest x2 5.46 us: local(): jnp.take(chol, fields[:, :, 0], axis=0)]
    reshape x0 -> x3, local copies, waits for them, and re-layouts: none -> 5.31 us  [the longest x2 4.36 us: local(): got = got.reshape(2, 2, 4, 2, 8, 2, 8, 8)]
  transfers between devices with their start and end apart: 5 -> 0, of which waited for: 4 -> 0; matrix products, arithmetic and copies ran while one was open for 17% -> 0% of each run, Pallas kernels for 0% -> 0%
where the time goes in v1:
time: 98.1 us; the launch traced here: 97.5 us
  Pallas kernels  90.8 us (93%)
  local copies, waits for them, and re-layouts  6.69 us (7%)
    pallas_call x1, Pallas kernels, ladder(): pl.pallas_call(ladder_kernel, out_shape=jax.ShapeDtypeStruct((N_VEC, 16,...  88 us
    reshape x2, local copies, waits for them, and re-layouts, local(): got = got.reshape(2, 2, 4, 2, 8, 2, 8, 8)  4.36 us
    pallas_call x1, Pallas kernels, compact(): pl.pallas_call(compact_kernel, out_shape=jax.ShapeDtypeStruct(((TASKS + 1...  2.84 us

profile of v1, /device:TPU:1, one launch (start us, length us, event | category | flops | bytes accessed | tf_op | source)
XLA Modules:
  0.0 97.5 jit_solution(2728912588606071167)
XLA Ops:
  0.0 1.4 %copy.7.list_ref = s32[64,4]{1,0:T(8,128)} copy(s32[64,4]{0,1:T(4,128)} %param.6) | data formatting | bytes 2048 | tf_op args[2]
  1.4 2.8 %shard_map.46.task_ref = s32[132]{0:T(256)} custom-call(s32[64,4]{1,0:T(8,128)} %copy.7.list_ref, s32[32]{0:T(128)} %counts_ref.1), custom_call_target="tpu_custom_call" | custom-call | tf_op jit(solution)/shard_map/pallas_call | solution.py:30
  4.2 88.0 %shard_map.47 = bf16[16,16,128]{2,1,0:T(8,128)(2,1)} custom-call(s32[132]{0:T(256)} %shard_map.46.task_ref, bf16[64,32,512]{2,1,0:T(8,128)(2,1)} %chol_hbm.1, bf16[64,8,1024]{2,1,0:T(8,128)(2,1)} %amp_hbm.1), custom_call_target="tpu_custom_call" | custom-call | tf_op jit(solution)/shard_map/pallas_call | solution.py:267
  92.2 2.2 %reshape.6 = bf16[2,2,4,2,8,2,8,8]{7,6,5,4,3,2,1,0:T(8,128)(2,1)S(1)} reshape(bf16[16,16,128]{2,1,0:T(8,128)(2,1)} %shard_map.47) | data formatting | bytes 131072 | tf_op jit(solution)/shard_map/reshape | solution.py:312
  94.4 2.2 %copy.8 = bf16[2,2,4,2,8,2,8,8]{4,1,6,0,7,2,3,5:T(2,128)(2,1)S(1)} copy(bf16[2,2,4,2,8,2,8,8]{7,6,5,4,3,2,1,0:T(8,128)(2,1)S(1)} %reshape.6) | data formatting | bytes 131072 | tf_op jit(solution)/shard_map/reshape | solution.py:312
  96.6 0.9 copy.9

commit v2 on v1

--- a/solution.py
+++ b/solution.py
@@ -18,12 +18,15 @@
 
 
 def compact_kernel(list_ref, counts_ref, out_ref):
-    def entry(e, position):
+    def one_list(w, position):
         for k in range(4):
-            out_ref[position * 4 + k] = list_ref[e, k]
-        return position + jnp.where(lax.rem(e, MOST) < counts_ref[e // MOST], 1, 0)
-
-    lax.fori_loop(0, N_AMP * MOST, entry, 0)
+            out_ref[position * 4 + k] = list_ref[k, w * MOST]
+        position = position + jnp.minimum(counts_ref[w], 1)
+        for k in range(4):
+            out_ref[position * 4 + k] = list_ref[k, w * MOST + 1]
+        return position + jnp.maximum(counts_ref[w] - 1, 0)
+
+    lax.fori_loop(0, N_AMP, one_list, 0)
 
 
 def compact(task_list, counts):
@@ -45,7 +48,7 @@
 
 def ladder_kernel(
     task_ref, chol_hbm, amp_hbm, out_ref,
-    chol_v, amp_v, xs, ys, ts, xr, yr, tr, xp, tfull, qs, vs, vr, ssum, keys, s2s, s2r, s3s, s3r,
+    chol_v, amp_v, xs, ys, ts, xr, yr, tr, xp, tfull, qs, order, vs, vr, ssum, keys, s2s, s2r, s3s, s3r,
     in_sem, x_send, x_recv, y_send, y_recv, t_send, t_recv, tv_send, tv_recv,
     v_send, v_recv, s2_send, s2_recv, s3_send, s3_recv,
 ):
@@ -54,11 +57,25 @@
     y, x_hi = v // 2, v % 2
     x_lo, z, core = m // 16, (m // 2) % 8, m % 2
 
-    def amp_peer(j):
-        return ((x_lo + (j // 2) % 2) % 2) * 16 + ((z + shift_of(j // 4) + 8) % 8) * 2 + (core + j) % 2
-
-    def vec_peer(j):
-        return (v + j) % N_VEC
+    x_of = [x_lo * 16, (1 - x_lo) * 16]
+    z_of = [(z + step) % 8 * 2 for step in (0, 7, 1, 6, 2, 5, 3, 4)]
+    core_of = [core, 1 - core]
+    y_of = [(y + step) % 8 * 2 for step in (0, 7, 1, 6, 2, 5, 3, 4)]
+    hi_of = [x_hi, 1 - x_hi]
+
+    def amp_peers(groups):
+        for q in groups:
+            for dx, dc in ((1, 1), (1, 0), (0, 1), (0, 0)):
+                if q or dx or dc:
+                    yield q, x_of[dx] + z_of[q] + core_of[dc]
+
+    def vec_peers():
+        for q in range(7, -1, -1):
+            for dh in (1, 0):
+                if q or dh:
+                    yield y_of[q] + hi_of[dh]
+
+    near, far = range(8), range(7, -1, -1)
 
     def to_amp(src, dst, send, recv, peer):
         pltpu.make_async_remote_copy(
@@ -79,13 +96,10 @@
 
     barrier = pltpu.get_barrier_semaphore()
 
-    @pl.loop(1, N_AMP)
-    def _(j):
-        pl.semaphore_signal(barrier, inc=1, device_id={"amp": amp_peer(j)}, device_id_type=MESH)
-
-    @pl.loop(1, N_VEC)
-    def _(j):
-        pl.semaphore_signal(barrier, inc=1, device_id={"vec": vec_peer(j)}, device_id_type=MESH)
+    for _, peer in amp_peers(far):
+        pl.semaphore_signal(barrier, inc=1, device_id={"amp": peer}, device_id_type=MESH)
+    for peer in vec_peers():
+        pl.semaphore_signal(barrier, inc=1, device_id={"vec": peer}, device_id_type=MESH)
 
     load_amp.wait()
     columns = pl.ds(pl.multiple_of(y * 128, 128), 128)
@@ -107,30 +121,23 @@
     def _():
         pltpu.make_async_copy(ts.at[m], tr.at[v, m // 2], t_recv).start()
 
-        @pl.loop(1, N_AMP)
-        def _(j):
-            peer = amp_peer(j)
+        for _, peer in amp_peers(far):
             to_amp(ts.at[peer], tr.at[v, m // 2], t_send, t_recv, peer)
 
     pltpu.make_async_copy(xs.at[m], xr.at[m], x_recv).start()
 
-    @pl.loop(1, N_AMP)
-    def _(j):
-        peer = amp_peer(j)
+    for _, peer in amp_peers(near):
         to_amp(xs.at[peer], xr.at[m], x_send, x_recv, peer)
 
     pltpu.make_async_copy(ys.at[m], yr.at[x_lo, z, core], y_recv.at[0]).start()
 
-    @pl.loop(1, N_AMP)
-    def _(j):
-        peer = amp_peer(j)
-        to_amp(ys.at[peer], yr.at[x_lo, z, core], y_send, y_recv.at[j // 4], peer)
+    for q, peer in amp_peers(near):
+        to_amp(ys.at[peer], yr.at[x_lo, z, core], y_send, y_recv.at[q], peer)
 
     arrived(tr.at[v], t_recv)
 
-    @pl.loop(1, N_VEC)
-    def _(j):
-        to_vec(tr.at[v], tr.at[v], tv_send, tv_recv, vec_peer(j))
+    for peer in vec_peers():
+        to_vec(tr.at[v], tr.at[v], tv_send, tv_recv, peer)
 
     lane = lax.broadcasted_iota(jnp.int32, (8, 256), 1)
 
@@ -143,6 +150,10 @@
     def _(k):
         rows = lax.broadcasted_iota(jnp.int32, (128, 256), 0) + k * 128
         keys[pl.ds(pl.multiple_of(k * 128, 128), 128), :] = jnp.where(rows == wanted, 1.0, 0.0).astype(BF16)
+
+    rows = lax.broadcasted_iota(jnp.int32, (128, 128), 0)
+    cols = lax.broadcasted_iota(jnp.int32, (128, 128), 1)
+    order[...] = jnp.where(cols == (rows % 4) * 32 + rows // 4, 1.0, 0.0).astype(BF16)
 
     arrived(xr, x_recv)
 
@@ -171,7 +182,7 @@
 
     @pl.loop(0, 8)
     def _(q):
-        from_z = (z - shift_of(q) + 8) % 8
+        from_z = (z + shift_of(q) + 8) % 8
         arrived(yr.at[0, pl.ds(0, 2)], y_recv.at[q])
         y_rows = jnp.concatenate(
             [yr[0, from_z].reshape(64, 512), yr[1, from_z].reshape(64, 512)], axis=0
@@ -194,26 +205,28 @@
             for b in range(4):
                 qs[b * 32 : b * 32 + 32, k * 128 : k * 128 + 128] = w[b].astype(BF16)
         term = lax.dot_general(qs[...], tfull[...], NT, preferred_element_type=F32)
+        term = jnp.dot(order[...], term.astype(BF16), preferred_element_type=F32)
         for k in range(N_VEC):
             vs[q, k] = term[k * 8 : k * 8 + 8].astype(BF16)
 
         pltpu.make_async_copy(vs.at[q, v], vr.at[q, v], v_recv.at[q]).start()
 
-        @pl.loop(1, N_VEC)
-        def _(j):
-            peer = vec_peer(j)
+        for peer in vec_peers():
             to_vec(vs.at[q, peer], vr.at[q, v], v_send.at[q], v_recv.at[q], peer)
 
     @pl.loop(0, 8)
     def _(q):
-        from_z = (z - shift_of(q) + 8) % 8
+        from_z = (z + shift_of(q) + 8) % 8
         arrived(vr.at[q], v_recv.at[q])
         total = vr[q, 0].astype(F32)
         for k in range(1, N_VEC):
             total += vr[q, k].astype(F32)
         high = total.astype(BF16).astype(F32)
-        ssum[pl.ds(pl.multiple_of(from_z * 8, 8), 8), :] = high
-        ssum[pl.ds(pl.multiple_of(from_z * 8 + 64, 8), 8), :] = total - high
+        low = total - high
+        for k in range(8):
+            row = (k // 4) * 32 + ((k // 2) % 2) * 16 + from_z * 2 + k % 2
+            ssum[pl.ds(row, 1), :] = high[k : k + 1]
+            ssum[pl.ds(row + 64, 1), :] = low[k : k + 1]
 
     turned = ssum[...].T
     for k in range(N_AMP):
@@ -221,9 +234,7 @@
 
     pltpu.make_async_copy(s2s.at[m], s2r.at[m], s2_recv).start()
 
-    @pl.loop(1, N_AMP)
-    def _(j):
-        peer = amp_peer(j)
+    for _, peer in amp_peers(far):
         to_amp(s2s.at[peer], s2r.at[m], s2_send, s2_recv, peer)
 
     arrived(s2r, s2_recv)
@@ -238,13 +249,16 @@
 
     pltpu.make_async_copy(s3s.at[v], s3r.at[v], s3_recv).start()
 
-    @pl.loop(1, N_VEC)
-    def _(j):
-        peer = vec_peer(j)
+    for peer in vec_peers():
         to_vec(s3s.at[peer], s3r.at[v], s3_send, s3_recv, peer)
 
     arrived(s3r, s3_recv)
-    out_ref[...] = s3r[...]
+    for k in range(0, N_VEC, 2):
+        left, right = s3r[k].astype(F32), s3r[k + 1].astype(F32)
+        upper = jnp.where(low16, left, pltpu.roll(right, 64, 1)).astype(BF16)
+        lower = jnp.where(low16, pltpu.roll(left, 64, 1), right).astype(BF16)
+        for p, rows in enumerate((upper[:8], upper[8:], lower[:8], lower[8:])):
+            out_ref[p, :, k * 64 : k * 64 + 128] = rows
 
     @pl.when(core == x_hi)
     def _():
@@ -266,7 +280,7 @@
     dma = pltpu.SemaphoreType.DMA
     return pl.pallas_call(
         ladder_kernel,
-        out_shape=jax.ShapeDtypeStruct((N_VEC, 16, 128), BF16),
+        out_shape=jax.ShapeDtypeStruct((4, 8, PAIRS), BF16),
         in_specs=[
             pl.BlockSpec(memory_space=pltpu.SMEM),
             pl.BlockSpec(memory_space=pl.ANY),
@@ -285,6 +299,7 @@
             pltpu.VMEM((1024, 512), BF16),
             pltpu.VMEM((256, 1024), BF16),
             pltpu.VMEM((128, 1024), BF16),
+            pltpu.VMEM((128, 128), BF16),
             pltpu.VMEM((8, 16, 8, 256), BF16),
             pltpu.VMEM((8, 16, 8, 256), BF16),
             pltpu.VMEM((128, 256), F32),
@@ -307,10 +322,7 @@
 
 
 def local(chol, amplitudes, task_list, counts):
-    tasks = compact(task_list, counts)
-    got = ladder(tasks, chol, amplitudes)
-    got = got.reshape(2, 2, 4, 2, 8, 2, 8, 8)
-    return got.transpose(5, 3, 4, 2, 7, 0, 6, 1).reshape(4, 8, PAIRS)
+    return ladder(compact(task_list.T, counts), chol, amplitudes)
 
 
 def solution(mesh):

time: 98.1 us -> 88.6 us (0.903)
  local copies, waits for them, and re-layouts: 6.69 us -> 1.47 us
  Pallas kernels: 90.8 us -> 86.9 us
    reshape x3 -> x0, local copies, waits for them, and re-layouts: 5.31 us -> none  [the longest x2 4.36 us: local(): got = got.reshape(2, 2, 4, 2, 8, 2, 8, 8)]
    pallas_call x1, Pallas kernels: 88 us -> 85 us  [ladder(): pl.pallas_call(ladder_kernel, out_shape=jax.ShapeDtypeStruct((4, 8, PAIRS...]
where the time goes in v2:
time: 88.6 us; the launch traced here: 88.4 us
  Pallas kernels  86.9 us (98%)
  local copies, waits for them, and re-layouts  1.47 us (2%)
    pallas_call x1, Pallas kernels, ladder(): pl.pallas_call(ladder_kernel, out_shape=jax.ShapeDtypeStruct((4, 8, PAIRS...  85 us
    pallas_call x1, Pallas kernels, compact(): pl.pallas_call(compact_kernel, out_shape=jax.ShapeDtypeStruct(((TASKS + 1...  1.87 us

profile of v2, /device:TPU:1, one launch (start us, length us, event | category | flops | bytes accessed | tf_op | source)
XLA Modules:
  0.0 88.4 jit_solution(7900111681910908206)
XLA Ops:
  0.0 1.9 %shard_map.46.task_ref = s32[132]{0:T(256)} custom-call(s32[4,64]{1,0:T(4,128)} %bitcast.1, s32[32]{0:T(128)} %counts_ref.1), custom_call_target="tpu_custom_call" | custom-call | tf_op jit(solution)/shard_map/pallas_call | solution.py:33
  1.9 85.0 %shard_map.47 = bf16[4,8,1024]{2,1,0:T(8,128)(2,1)} custom-call(s32[132]{0:T(256)} %shard_map.46.task_ref, bf16[64,32,512]{2,1,0:T(8,128)(2,1)} %chol_hbm.1, bf16[64,8,1024]{2,1,0:T(8,128)(2,1)} %amp_hbm.1), custom_call_target="tpu_custom_call" | custom-call | tf_op jit(solution)/shard_map/pallas_call | solution.py:281
  86.9 1.5 %copy.6 = bf16[4,8,1024]{2,1,0:T(8,128)(2,1)} copy(bf16[4,8,1024]{2,1,0:T(8,128)(2,1)} %shard_map.47) | data formatting | bytes 131072

commit v3 on v2

--- a/solution.py
+++ b/solution.py
@@ -48,7 +48,7 @@
 
 def ladder_kernel(
     task_ref, chol_hbm, amp_hbm, out_ref,
-    chol_v, amp_v, xs, ys, ts, xr, yr, tr, xp, tfull, qs, order, vs, vr, ssum, keys, s2s, s2r, s3s, s3r,
+    out_v, chol_v, amp_v, xs, ys, ts, xr, yr, tr, xp, tfull, qs, order, vs, vr, ssum, keys, s2s, s2r, s3s, s3r,
     in_sem, x_send, x_recv, y_send, y_recv, t_send, t_recv, tv_send, tv_recv,
     v_send, v_recv, s2_send, s2_recv, s3_send, s3_recv,
 ):
@@ -258,7 +258,9 @@
         upper = jnp.where(low16, left, pltpu.roll(right, 64, 1)).astype(BF16)
         lower = jnp.where(low16, pltpu.roll(left, 64, 1), right).astype(BF16)
         for p, rows in enumerate((upper[:8], upper[8:], lower[:8], lower[8:])):
-            out_ref[p, :, k * 64 : k * 64 + 128] = rows
+            out_v[p, :, k * 64 : k * 64 + 128] = rows
+    store = pltpu.make_async_copy(out_v, out_ref, in_sem.at[0])
+    store.start()
 
     @pl.when(core == x_hi)
     def _():
@@ -274,6 +276,7 @@
 
     arrived(s2s.at[pl.ds(0, N_AMP - 1)], s2_send)
     arrived(s3s.at[pl.ds(0, N_VEC - 1)], s3_send)
+    store.wait()
 
 
 def ladder(tasks, chol, amplitudes):
@@ -286,8 +289,9 @@
             pl.BlockSpec(memory_space=pl.ANY),
             pl.BlockSpec(memory_space=pl.ANY),
         ],
-        out_specs=pl.BlockSpec(memory_space=pltpu.VMEM),
+        out_specs=pl.BlockSpec(memory_space=pl.ANY),
         scratch_shapes=[
+            pltpu.VMEM((4, 8, PAIRS), BF16),
             pltpu.VMEM((64, 32, 512), BF16),
             pltpu.VMEM((64, 8, 1024), BF16),
             pltpu.VMEM((32, 32, 512), BF16),
@@ -317,7 +321,7 @@
             dma(()), dma(()),
             dma(()), dma(()),
         ],
-        compiler_params=pltpu.CompilerParams(collective_id=0, has_side_effects=True),
+        compiler_params=pltpu.CompilerParams(collective_id=0, has_side_effects=True, vmem_limit_bytes=55000 * 2**10),
     )(tasks, chol, amplitudes)
 
 

time: 88.6 us -> 87.7 us (0.990)
  no operation moved by 1% of the time
where the time goes in v3:
time: 87.7 us; the launch traced here: 87.6 us
  Pallas kernels  86.2 us (98%)
  local copies, waits for them, and re-layouts  1.31 us (1%)
    pallas_call x1, Pallas kernels, ladder(): pl.pallas_call(ladder_kernel, out_shape=jax.ShapeDtypeStruct((4, 8, PAIRS...  84.4 us
    pallas_call x1, Pallas kernels, compact(): pl.pallas_call(compact_kernel, out_shape=jax.ShapeDtypeStruct(((TASKS + 1...  1.87 us

profile of v3, /device:TPU:1, one launch (start us, length us, event | category | flops | bytes accessed | tf_op | source)
XLA Modules:
  0.0 87.6 jit_solution(14543771705419033241)
XLA Ops:
  0.0 1.9 %shard_map.46.task_ref = s32[132]{0:T(256)} custom-call(s32[4,64]{1,0:T(4,128)} %bitcast.1, s32[32]{0:T(128)} %counts_ref.1), custom_call_target="tpu_custom_call" | custom-call | tf_op jit(solution)/shard_map/pallas_call | solution.py:33
  1.9 0.0 copy-start
  1.9 0.7 copy-done
  2.6 84.4 %shard_map.47 = bf16[4,8,1024]{2,1,0:T(8,128)(2,1)S(1)} custom-call(s32[132]{0:T(256)S(1)} %copy-done, bf16[64,32,512]{2,1,0:T(8,128)(2,1)} %chol_hbm.1, bf16[64,8,1024]{2,1,0:T(8,128)(2,1)} %amp_hbm.1), custom_call_target="tpu_custom_call" | custom-call | tf_op jit(solution)/shard_map/pallas_call | solution.py:284
  86.9 0.6 copy.6
Async XLA Ops:
  1.9 0.7 copy-start
